TPU v7x, 128 devices: a whole 4x4x4 slice. The times are simulated.
128 devices in a mesh: rep: 32 (over z, y, core), tensor: 4 (over x).
Axes of the slice: x: 4, y: 4, z: 4, core: 2. Of those that a mesh axis runs over, the one named last changes fastest.
Arguments:
- hidden_in: bfloat16 [2048, 4096], P('rep', 'tensor'), may hold values from -25 to 25
- query: bfloat16 [2048, 4096], P('rep', 'tensor'), may hold values from -6 to 6
- new_kv: bfloat16 [2048, 2, 512], P('rep', None, 'tensor'), may hold values from -8 to 8
- pool: bfloat16 [4096, 128, 2, 512], P('rep', None, None, 'tensor'), may hold values from -8 to 8
- page_table: int32 [2048, 2], P('rep'), may hold values from 0 to 127, as said below
- lengths: int32 [2048], replicated, may hold values from 1 to 256, 262144 in all
- dest: int32 [32], replicated, may hold values from 0 to 31, each once
- out_weight: bfloat16 [4096, 4096], P('tensor'), may hold values from -0.1875 to 0.1875
- norm_gain: float32 [4096], P('tensor'), may hold values from 0.1 to 1.9
- gate_up: bfloat16 [4096, 2, 11008], P('tensor', None, 'rep'), may hold values from -0.09375 to 0.09375
- down_weight: bfloat16 [11008, 4096], P('rep', 'tensor'), may hold values from -0.109375 to 0.109375
Outputs:
- layer_out: bfloat16 [2048, 4096], P('rep', 'tensor')
Inputs may be any that keep to these rules, and one draw needn't show every extreme that they name: `page_table`: within a group no two requests share a page.
All inputs are finite; a program needn't handle non-finite values.
Results may differ from a plain program's by a relative error of at most 0.03.
Values may be sent and summed in bfloat16 or wider, within the bound.
No kernel may reach another device: no remote copies, remote signals or barrier semaphores. Data moves between devices by JAX's collectives and lax.ppermute only.
A program may use at most 128 MiB of HBM per device.

v0:
```python
import jax
import jax.numpy as jnp
from jax import lax
from jax.sharding import PartitionSpec as P

D = 4096
HD = 128
EPSILON = 1e-05


def attend(queries, cache_block, new_pair, counts):
    row_count = cache_block.shape[0]
    cache_len = cache_block.shape[1]
    kv_width = cache_block.shape[3]
    kv_heads = kv_width // HD
    group_size = queries.shape[1] // kv_width
    query_heads = queries.reshape(row_count, kv_heads, group_size, HD)
    key_heads = cache_block[:, :, 0].reshape(row_count, cache_len, kv_heads, HD)
    value_heads = cache_block[:, :, 1].reshape(row_count, cache_len, kv_heads, HD)
    new_key = new_pair[:, 0].reshape(row_count, kv_heads, HD)
    new_value = new_pair[:, 1].reshape(row_count, kv_heads, HD)
    score_scale = HD ** (-0.5)
    scores = (
        jnp.einsum("nkgd,nlkd->nkgl", query_heads, key_heads, preferred_element_type=jnp.float32)
        * score_scale
    )
    own_score = (
        jnp.einsum("nkgd,nkd->nkg", query_heads, new_key, preferred_element_type=jnp.float32)
        * score_scale
    )
    in_range = (jnp.arange(cache_len, dtype=jnp.int32)[None, :] < counts[:, None])[:, None, None, :]
    masked = jnp.where(in_range, scores, -jnp.inf)
    peak_score = jnp.maximum(jnp.max(masked, axis=-1), own_score)
    weights = jnp.where(in_range, jnp.exp(scores - peak_score[..., None]), 0.0)
    own_weight = jnp.exp(own_score - peak_score)
    denominator = jnp.sum(weights, axis=-1) + own_weight
    weighted = jnp.einsum(
        "nkgl,nlkd->nkgd",
        weights.astype(jnp.bfloat16),
        value_heads,
        preferred_element_type=jnp.float32,
    )
    weighted = weighted + jnp.einsum(
        "nkg,nkd->nkgd",
        own_weight.astype(jnp.bfloat16),
        new_value,
        preferred_element_type=jnp.float32,
    )
    return (weighted / denominator[..., None]).astype(jnp.bfloat16).reshape(row_count, -1)


def local(
    hidden_in,
    query,
    new_kv,
    pool,
    page_table,
    lengths,
    dest,
    out_weight,
    norm_gain,
    gate_up,
    down_weight,
):
    rows_here = hidden_in.shape[0]
    group_count = lax.axis_size("rep")
    my_group = lax.axis_index("rep")
    group_ids = jnp.arange(group_count, dtype=jnp.int32)
    source = jnp.sum(jnp.where(dest == my_group, group_ids, 0))
    page_count = page_table.shape[1]
    page_len = pool.shape[1]
    kv_width = pool.shape[3]
    cache_rows = pool[page_table].reshape(rows_here, page_count * page_len, 2, kv_width)
    my_lengths = lax.dynamic_slice_in_dim(lengths, my_group * rows_here, rows_here)
    home_attn = attend(query, cache_rows, new_kv, my_lengths)
    every_attn, every_hidden = (
        lax.all_gather(home_attn[-1:], "rep", axis=0, tiled=True),
        lax.all_gather(hidden_in[-1:], "rep", axis=0, tiled=True),
    )
    attention = jnp.concatenate(
        [home_attn[:-1], lax.dynamic_slice_in_dim(every_attn, source, 1)], axis=0
    )
    served = jnp.concatenate(
        [hidden_in[:-1], lax.dynamic_slice_in_dim(every_hidden, source, 1)], axis=0
    )
    projected = jnp.dot(attention, out_weight, preferred_element_type=jnp.float32)
    head_total = lax.psum_scatter(
        projected.astype(jnp.bfloat16), "tensor", scatter_dimension=1, tiled=True
    ).astype(jnp.float32)
    residual = served.astype(jnp.float32) + head_total
    square_sum = lax.psum(jnp.sum(residual * residual, axis=1), "tensor")
    normed = (residual * lax.rsqrt(square_sum / D + EPSILON)[:, None] * norm_gain[None, :]).astype(
        jnp.bfloat16
    )
    unit_count = gate_up.shape[2]
    flat_weight = gate_up.reshape(gate_up.shape[0], 2 * unit_count)
    partial_units = jnp.dot(
        lax.all_gather(normed, "rep", axis=0, tiled=True),
        flat_weight,
        preferred_element_type=jnp.float32,
    )
    partial_units = partial_units.reshape(partial_units.shape[0], 2, unit_count)
    unit_total = lax.psum(partial_units.astype(jnp.bfloat16), "tensor").astype(jnp.float32)
    activated = (jax.nn.silu(unit_total[:, 0]) * unit_total[:, 1]).astype(jnp.bfloat16)
    mixed = lax.psum_scatter(
        jnp.dot(activated, down_weight, preferred_element_type=jnp.float32).astype(jnp.bfloat16),
        "rep",
        scatter_dimension=0,
        tiled=True,
    ).astype(jnp.float32)
    return (residual + mixed).astype(jnp.bfloat16)


def solution(mesh):
    return jax.shard_map(
        local,
        mesh=mesh,
        in_specs=(
            P("rep", "tensor"),
            P("rep", "tensor"),
            P("rep", None, "tensor"),
            P("rep", None, None, "tensor"),
            P("rep", None),
            P(),
            P(),
            P("tensor", None),
            P("tensor"),
            P("tensor", None, "rep"),
            P("rep", "tensor"),
        ),
        out_specs=P("rep", "tensor"),
        check_vma=False,
    )
```

profile of v0, /device:TPU:0, one launch (start us, length us, event | category | flops | bytes accessed | tf_op | source)
XLA Modules:
  0.0 336.0 jit_solution(7279921076718886438)
XLA Ops:
  6.5 0.8 compare_select_fusion
  7.3 0.1 copy.17
  7.4 0.1 reshape.104
  7.6 23.2 %gather_fusion = bf16[128,128,2,128]{3,2,1,0:T(2,128)(2,1)} fusion(bf16[128,128,2,128]{3,2,1,0:T(2,128)(2,1)} %param.14, s32[1024]{0:T(1024)S(1)} %pad_clamp_fusion), kind=kCustom, calls=%fused_computation | custom fusion | bytes 16777728 | tf_op jit(solution)/shard_map/gather | solution.py:73
  30.8 8.9 %copy.18 = bf16[128,128,2,128]{3,1,0,2:T(8,128)(2,1)} copy(bf16[128,128,2,128]{3,2,1,0:T(2,128)(2,1)} %gather_fusion) | data formatting | bytes 16777216 | tf_op jit(solution)/shard_map/gather | solution.py:73
  39.7 0.8 dynamic_slice.10
  40.4 0.1 iota_compare_fusion
  40.6 0.2 fusion.22
  40.8 3.5 %select_reduce_fusion = (f32[64,8]{1,0:T(8,128)S(1)}, f32[64,256,8]{1,2,0:T(8,128)S(1)}) fusion(pred[64,256]{1,0:T(8,128)(4,1)S(1)} %iota_compare_fusion, bf16[64,8,128]{2,1,0:T(8,128)(2,1)S(1)} %bitcast.79, bf16[64,256,2,128]{3,1,0,2:T(8,128)(2,1)} %bitcast.68), kind=kOutput, calls=%fused_computation.23 | convolution fusion | flops 33947136 | bytes 4868096 | tf_op jit(solution)/shard_map/nkgd,nlkd->nkgl/dot_general | solution.py:24
  44.3 0.3 bitcast_reduce_fusion
  44.6 2.9 fusion.15
  47.5 26.2 %all-gather.1 = bf16[32,1,1024]{2,1,0:T(2,128)(2,1)S(1)} all-gather(bf16[1,1,1024]{2,1,0:T(2,128)(2,1)S(1)} %reshape.115), channel_id=1, replica_groups=mesh['rep'=32,'tensor'=4] {'rep'}, dimensions={0}, use_global_device_ids=true | all-gather | bytes 67584 | tf_op jit(solution)/shard_map/all_gather | solution.py:77
  73.7 0.6 fusion.25
  76.4 5.8 %convolution_convert_fusion = bf16[64,4096]{1,0:T(8,128)(2,1)} fusion(bf16[1024,4096]{1,0:T(8,128)(2,1)} %param.18, bf16[1,1024]{1,0:T(2,128)(2,1)S(1)} %dynamic-slice_bitcast_fusion, bf16[63,1024]{1,0:T(8,128)(2,1)S(1)} %bitcast.73), kind=kOutput, calls=%fused_computation.1 | convolution fusion | flops 537395200 | bytes 9043968 | tf_op jit(solution)/shard_map/dot_general | solution.py:86
  82.2 0.0 reduce-scatter.3.cloned.1.call-update
  82.2 0.0 all-gather.4.cloned.1.call-start
  82.3 24.0 %all-gather = bf16[32,1,1024]{2,1,0:T(2,128)(2,1)S(1)} all-gather(bf16[1,1,1024]{2,1,0:T(2,128)(2,1)S(1)} %slice_bitcast_fusion.14), channel_id=1, replica_groups=mesh['rep'=32,'tensor'=4] {'rep'}, dimensions={0}, use_global_device_ids=true | all-gather | bytes 67584 | tf_op jit(solution)/shard_map/all_gather | solution.py:78
  106.3 1.1 multiply_reduce_fusion
  107.4 10.5 %psum.14 = f32[64]{0:T(128)S(1)} all-reduce(f32[64]{0:T(128)S(1)} %multiply_reduce_fusion), channel_id=1, replica_groups=mesh['rep'=32,'tensor'=4] {'tensor'}, use_global_device_ids=true, to_apply=%region_5.6 | all-reduce | flops 64 | bytes 512 | tf_op jit(solution)/shard_map/psum | solution.py:91
  117.9 1.7 multiply_convert_fusion
  119.6 0.0 all-gather.4.cloned.1.call-update
  119.6 0.0 all-reduce.2.cloned.1.call-start
  119.6 42.7 %all-gather.4.cloned.1.call-done = bf16[2048,1024]{1,0:T(8,128)(2,1)} async-done(((bf16[64,1024]{1,0:T(8,128)(2,1)}), bf16[2048,1024]{1,0:T(8,128)(2,1)}) %all-gather.4.cloned.1.call-update) | async-done | bytes 4194320 | tf_op jit(solution)/shard_map/all_gather | solution.py:98
  162.3 6.7 %fusion.4 = bf16[2048,2,344]{0,2,1:T(8,128)(2,1)} fusion(bf16[2048,1024]{1,0:T(8,128)(2,1)} %all-gather.4.cloned.1.call-done, bf16[1024,2,344]{0,2,1:T(8,128)(2,1)S(1)} %copy-done), kind=kOutput, calls=%fused_computation.9 | convolution fusion | flops 2887090176 | bytes 8421376 | tf_op jit(solution)/shard_map/dot_general | solution.py:97
  169.0 0.0 all-reduce.2.cloned.1.call-update
  169.0 0.2 reduce-scatter.5.cloned.1.call-start
  169.3 69.5 %all-reduce.2.cloned.1.call-done = bf16[2048,2,344]{0,2,1:T(8,128)(2,1)} async-done(((bf16[2048,2,344]{0,2,1:T(8,128)(2,1)}), bf16[2048,2,344]{0,2,1:T(8,128)(2,1)}) %all-reduce.2.cloned.1.call-update) | async-done | bytes 2818064 | tf_op jit(solution)/shard_map/psum | solution.py:103
  238.8 2.5 convert_element_type.50
  241.3 4.4 %convolution_convert_fusion.1 = bf16[2048,1024]{1,0:T(8,128)(2,1)} fusion(bf16[344,1024]{1,0:T(8,128)(2,1)S(1)} %copy-done.6, f32[2048,2,344]{0,2,1:T(8,128)S(1)} %convert_element_type.50), kind=kOutput, calls=%fused_computation.8 | convolution fusion | flops 1449164800 | bytes 10534912 | tf_op jit(solution)/shard_map/dot_general | solution.py:106
  245.8 0.0 reduce-scatter.5.cloned.1.call-update
  245.8 82.1 %reduce-scatter.5.cloned.1.call-done = bf16[64,1024]{1,0:T(8,128)(2,1)} async-done(((bf16[2048,1024]{1,0:T(8,128)(2,1)}), bf16[64,1024]{1,0:T(8,128)(2,1)}) %reduce-scatter.5.cloned.1.call-update) | async-done | bytes 131088 | tf_op jit(solution)/shard_map/reduce_scatter | solution.py:105
  327.9 1.6 add_convert_fusion
  (33 shorter events, 0.2 us)
Async XLA Ops:
  6.5 155.8 %copy-start = (bf16[1024,2,344]{0,2,1:T(8,128)(2,1)S(1)}, bf16[1024,2,344]{0,2,1:T(8,128)(2,1)}, u32[]{:S(2)}) copy-start(bf16[1024,2,344]{0,2,1:T(8,128)(2,1)} %param.20) | copy-start | bytes 4227076
  6.5 99.8 %reduce-scatter.3.cloned.1.call-start = ((), (), s32[]{:S(2)}) async-start(), calls=%async_computation.2 | async-start | bytes 655360 | tf_op jit(solution)/shard_map/reduce_scatter | solution.py:87
  30.8 9.7 %copy-start.3 = (bf16[64,1024]{1,0:T(8,128)(2,1)S(1)}, bf16[64,1024]{1,0:T(8,128)(2,1)}, u32[]{:S(2)}) copy-start(bf16[64,1024]{1,0:T(8,128)(2,1)} %param.12) | copy-start | bytes 393220
  30.8 9.8 %copy-start.4 = (bf16[64,2,128]{2,1,0:T(2,128)(2,1)S(1)}, bf16[64,2,128]{2,1,0:T(2,128)(2,1)}, u32[]{:S(2)}) copy-start(bf16[64,2,128]{2,1,0:T(2,128)(2,1)} %param.13) | copy-start | bytes 98308
  44.3 29.4 %copy-start.7 = (s32[32]{0:T(128)S(1)}, s32[32]{0:T(128)}, u32[]{:S(2)}) copy-start(s32[32]{0:T(128)} %param.17) | copy-start | bytes 388
  76.4 5.9 %copy-start.1 = (bf16[64,1024]{1,0:T(8,128)(2,1)S(1)}, bf16[64,1024]{1,0:T(8,128)(2,1)}, u32[]{:S(2)}) copy-start(bf16[64,1024]{1,0:T(8,128)(2,1)} %param.11) | copy-start | bytes 393220
  76.4 41.5 %copy-start.5 = (f32[1024]{0:T(1024)S(1)}, f32[1024]{0:T(1024)}, u32[]{:S(2)}) copy-start(f32[1024]{0:T(1024)} %param.19) | copy-start | bytes 12292
  82.2 80.1 %all-gather.4.cloned.1.call-start = ((), (), s32[]{:S(2)}) async-start(), calls=%async_computation.3 | async-start | bytes 4325376 | tf_op jit(solution)/shard_map/all_gather | solution.py:98
  119.6 119.2 %all-reduce.2.cloned.1.call-start = ((), (), s32[]{:S(2)}) async-start(), calls=%async_computation.4 | async-start | bytes 5636096 | tf_op jit(solution)/shard_map/psum | solution.py:103
  169.0 72.3 %copy-start.6 = (bf16[344,1024]{1,0:T(8,128)(2,1)S(1)}, bf16[344,1024]{1,0:T(8,128)(2,1)}, u32[]{:S(2)}) copy-start(bf16[344,1024]{1,0:T(8,128)(2,1)} %param.21) | copy-start | bytes 2113540
  169.0 158.8 %reduce-scatter.5.cloned.1.call-start = ((), (), s32[]{:S(2)}) async-start(), calls=%async_computation.5 | async-start | bytes 4325376 | tf_op jit(solution)/shard_map/reduce_scatter | solution.py:105
  245.8 82.1 %copy-start.2 = (bf16[64,1024]{1,0:T(8,128)(2,1)S(1)}, bf16[64,1024]{1,0:T(8,128)(2,1)}, u32[]{:S(2)}) copy-start(bf16[64,1024]{1,0:T(8,128)(2,1)} %reduce-scatter.3.cloned.1.call-done) | copy-start | bytes 393220
Sparse Core Ops, SparseCore 0:
  82.3 20.4 reduce-scatter.2
  119.7 42.5 all-gather.3
  169.1 69.5 all-reduce.1
  245.9 81.9 reduce-scatter.4
where the time goes:
time: 336 us
  waiting for transfers between devices  194 us (58%)
  blocking collectives  60.7 us (18%)
  local copies, waits for them, and re-layouts  33.2 us (10%)
  matrix products  23.4 us (7%)
  between operations  15.3 us (5%)
  other arithmetic  8.71 us (3%)
    reduce_scatter x1, waiting for transfers between devices, local(): lax.psum_scatter(jnp.dot(activated, down_weight, preferred_element_type=j...  82.1 us
    psum x1, waiting for transfers between devices, local(): lax.psum(partial_units.astype(jnp.bfloat16), 'tensor').astype(jnp.float32)  69.5 us
    all_gather x1, waiting for transfers between devices, local(): lax.all_gather(normed, 'rep', axis=0, tiled=True)  42.7 us
    gather x2, local copies, waits for them, and re-layouts, local(): pool[page_table].reshape(rows_here, page_count * page_len, 2, kv_width)  32.1 us
    all_gather x1, blocking collectives, local(): lax.all_gather(home_attn[-1:], 'rep', axis=0, tiled=True)  26.2 us
    all_gather x1, blocking collectives, local(): lax.all_gather(hidden_in[-1:], 'rep', axis=0, tiled=True)  24 us
    psum x1, blocking collectives, local(): square_sum = lax.psum(jnp.sum(residual * residual, axis=1), 'tensor')  10.5 us
  transfers between devices with their start and end apart: 4, of which 3 were waited for; matrix products, arithmetic and copies ran while one was open for 0% of the time, Pallas kernels for 0%

commit v1 on v0

--- a/solution.py
+++ b/solution.py
@@ -100,7 +100,9 @@
         preferred_element_type=jnp.float32,
     )
     partial_units = partial_units.reshape(partial_units.shape[0], 2, unit_count)
-    unit_total = lax.psum(partial_units.astype(jnp.bfloat16), "tensor").astype(jnp.float32)
+    unit_total = jnp.sum(
+        lax.all_gather(partial_units.astype(jnp.bfloat16), "tensor"), axis=0
+    ).astype(jnp.float32)
     activated = (jax.nn.silu(unit_total[:, 0]) * unit_total[:, 1]).astype(jnp.bfloat16)
     mixed = lax.psum_scatter(
         jnp.dot(activated, down_weight, preferred_element_type=jnp.float32).astype(jnp.bfloat16),

time: 336 us -> 419 us (1.25)
  waiting for transfers between devices: 194 us -> 233 us
  local copies, waits for them, and re-layouts: 33.2 us -> 57.8 us
  other arithmetic: 8.71 us -> 27.3 us
    all_gather x0 -> x1, waiting for transfers between devices: none -> 107 us  [local(): lax.all_gather(partial_units.astype(jnp.bfloat16), 'tensor')]
    psum x1 -> x0, waiting for transfers between devices: 69.5 us -> none  [local(): lax.psum(partial_units.astype(jnp.bfloat16), 'tensor').astype(jnp.float32)]
    all_gather x0 -> x1, local copies, waits for them, and re-layouts: none -> 23.7 us  [local(): lax.all_gather(partial_units.astype(jnp.bfloat16), 'tensor')]
    reduce_sum x0 -> x1, other arithmetic: none -> 17.7 us  [local(): jnp.sum(lax.all_gather(partial_units.astype(jnp.bfloat16), 'tensor'), axi...]
where the time goes in v1:
time: 419 us; the launch traced here: 418 us
  waiting for transfers between devices  233 us (56%)
  blocking collectives  60.7 us (14%)
  local copies, waits for them, and re-layouts  57.8 us (14%)
  other arithmetic  27.3 us (7%)
  matrix products  23.5 us (6%)
  between operations  15.3 us (4%)
    all_gather x1, waiting for transfers between devices, local(): lax.all_gather(partial_units.astype(jnp.bfloat16), 'tensor')  107 us
    reduce_scatter x1, waiting for transfers between devices, local(): lax.psum_scatter(jnp.dot(activated, down_weight, preferred_element_type=j...  83.2 us
    all_gather x1, waiting for transfers between devices, local(): lax.all_gather(normed, 'rep', axis=0, tiled=True)  42.7 us
    gather x2, local copies, waits for them, and re-layouts, local(): pool[page_table].reshape(rows_here, page_count * page_len, 2, kv_width)  32 us
    all_gather x1, blocking collectives, local(): lax.all_gather(home_attn[-1:], 'rep', axis=0, tiled=True)  26.2 us
    all_gather x1, blocking collectives, local(): lax.all_gather(hidden_in[-1:], 'rep', axis=0, tiled=True)  24 us
    all_gather x1, local copies, waits for them, and re-layouts, local(): lax.all_gather(partial_units.astype(jnp.bfloat16), 'tensor')  23.7 us
    reduce_sum x1, other arithmetic, local(): jnp.sum(lax.all_gather(partial_units.astype(jnp.bfloat16), 'tensor'), axi...  17.7 us
  transfers between devices with their start and end apart: 4, of which 3 were waited for; matrix products, arithmetic and copies ran while one was open for 0% of the time, Pallas kernels for 0%

profile of v1, /device:TPU:0, one launch (start us, length us, event | category | flops | bytes accessed | tf_op | source)
XLA Modules:
  0.0 417.5 jit_solution(3554288024206522005)
XLA Ops:
  6.5 0.8 compare_select_fusion
  7.3 0.8 dynamic_slice.10
  8.1 0.1 iota_compare_fusion
  8.2 0.1 copy.18
  8.3 0.1 reshape.104
  8.4 0.9 slice_convert_fusion
  9.3 0.9 copy.24
  10.3 23.2 %gather_fusion = bf16[128,128,2,128]{3,2,1,0:T(2,128)(2,1)} fusion(bf16[128,128,2,128]{3,2,1,0:T(2,128)(2,1)} %param.14, s32[1024]{0:T(1024)S(1)} %pad_clamp_fusion), kind=kCustom, calls=%fused_computation | custom fusion | bytes 16777728 | tf_op jit(solution)/shard_map/gather | solution.py:73
  33.4 8.9 %copy.19 = bf16[128,128,2,128]{3,1,0,2:T(8,128)(2,1)} copy(bf16[128,128,2,128]{3,2,1,0:T(2,128)(2,1)} %gather_fusion) | data formatting | bytes 16777216 | tf_op jit(solution)/shard_map/gather | solution.py:73
  42.3 0.2 fusion.22
  42.5 3.5 select_reduce_fusion
  46.0 0.3 bitcast_reduce_fusion
  46.3 2.9 fusion.15
  49.2 0.6 fusion.25
  51.2 26.2 %all-gather.2 = bf16[32,1,1024]{2,1,0:T(2,128)(2,1)S(1)} all-gather(bf16[1,1,1024]{2,1,0:T(2,128)(2,1)S(1)} %reshape.116), channel_id=1, replica_groups=mesh['rep'=32,'tensor'=4] {'rep'}, dimensions={0}, use_global_device_ids=true | all-gather | bytes 67584 | tf_op jit(solution)/shard_map/all_gather | solution.py:77
  78.1 5.8 %convolution_convert_fusion = bf16[64,4096]{1,0:T(8,128)(2,1)} fusion(bf16[1024,4096]{1,0:T(8,128)(2,1)} %param.18, bf16[1,1024]{1,0:T(2,128)(2,1)S(1)} %dynamic-slice_bitcast_fusion, bf16[63,1024]{1,0:T(8,128)(2,1)S(1)} %bitcast.75), kind=kOutput, calls=%fused_computation.1 | convolution fusion | flops 537395200 | bytes 9043968 | tf_op jit(solution)/shard_map/dot_general | solution.py:86
  83.9 0.0 all-gather.6.cloned.1.call-start
  84.0 24.0 %all-gather.1 = bf16[32,1,1024]{2,1,0:T(2,128)(2,1)S(1)} all-gather(bf16[1,1,1024]{2,1,0:T(2,128)(2,1)S(1)} %slice_bitcast_fusion.14), channel_id=1, replica_groups=mesh['rep'=32,'tensor'=4] {'rep'}, dimensions={0}, use_global_device_ids=true | all-gather | bytes 67584 | tf_op jit(solution)/shard_map/all_gather | solution.py:78
  108.0 1.1 multiply_reduce_fusion
  109.1 10.5 %psum.7 = f32[64]{0:T(128)S(1)} all-reduce(f32[64]{0:T(128)S(1)} %multiply_reduce_fusion), channel_id=1, replica_groups=mesh['rep'=32,'tensor'=4] {'tensor'}, use_global_device_ids=true, to_apply=%region_5.6 | all-reduce | flops 64 | bytes 512 | tf_op jit(solution)/shard_map/psum | solution.py:91
  119.6 1.7 multiply_convert_fusion
  121.3 0.0 all-gather.8.cloned.1.call-start
  121.3 42.7 %all-gather.6.cloned.1.call-done = bf16[2048,1024]{1,0:T(8,128)(2,1)} async-done(((bf16[64,1024]{1,0:T(8,128)(2,1)}), bf16[2048,1024]{1,0:T(8,128)(2,1)}) %all-gather.6.cloned.1.call-update) | async-done | bytes 4194320 | tf_op jit(solution)/shard_map/all_gather | solution.py:98
  164.1 6.7 %fusion.4 = bf16[2048,2,344]{0,2,1:T(8,128)(2,1)} fusion(bf16[2048,1024]{1,0:T(8,128)(2,1)} %all-gather.6.cloned.1.call-done, bf16[1024,2,344]{0,2,1:T(8,128)(2,1)S(1)} %copy-done), kind=kOutput, calls=%fused_computation.9 | convolution fusion | flops 2887090176 | bytes 8421376 | tf_op jit(solution)/shard_map/dot_general | solution.py:97
  170.8 0.2 reduce-scatter.5.cloned.1.call-start
  171.0 106.6 %all-gather.8.cloned.1.call-done = bf16[8192,2,344]{0,2,1:T(8,128)(2,1)} async-done(((bf16[2048,2,344]{0,2,1:T(8,128)(2,1)}), bf16[8192,2,344]{0,2,1:T(8,128)(2,1)}) %all-gather.8.cloned.1.call-update) | async-done | bytes 11272208 | tf_op jit(solution)/shard_map/all_gather | solution.py:104
  277.6 23.7 %reshape.110 = bf16[4,2048,2,344]{1,0,3,2:T(4,128)(2,1)} reshape(bf16[8192,2,344]{0,2,1:T(8,128)(2,1)} %all-gather.8.cloned.1.call-done) | data formatting | bytes 22544384 | tf_op jit(solution)/shard_map/all_gather | solution.py:104
  301.4 17.7 %reduce_sum.42 = bf16[2048,2,344]{0,2,1:T(8,128)(2,1)} reduce(bf16[4,2048,2,344]{1,0,3,2:T(4,128)(2,1)} %reshape.110, bf16[]{:T(256)} %constant.32.clone.1), dimensions={0}, to_apply=%region_6.7 | reduce | flops 4227072 | bytes 14090242 | tf_op jit(solution)/shard_map/reduce_sum | solution.py:103
  319.0 2.6 convert_element_type.52
  321.7 4.4 %convolution_convert_fusion.1 = bf16[2048,1024]{1,0:T(8,128)(2,1)} fusion(bf16[344,1024]{1,0:T(8,128)(2,1)S(1)} %copy-done.5, f32[2048,2,344]{0,2,1:T(8,128)S(1)} %convert_element_type.52), kind=kOutput, calls=%fused_computation.8 | convolution fusion | flops 1449164800 | bytes 10534912 | tf_op jit(solution)/shard_map/dot_general | solution.py:108
  326.1 83.2 %reduce-scatter.5.cloned.1.call-done = bf16[64,1024]{1,0:T(8,128)(2,1)} async-done(((bf16[2048,1024]{1,0:T(8,128)(2,1)}), bf16[64,1024]{1,0:T(8,128)(2,1)}) %reduce-scatter.5.cloned.1.call-update) | async-done | bytes 131088 | tf_op jit(solution)/shard_map/reduce_scatter | solution.py:107
  409.4 1.6 add_convert_fusion
  (33 shorter events, 0.2 us)
Async XLA Ops:
  6.5 157.5 %copy-start = (bf16[1024,2,344]{0,2,1:T(8,128)(2,1)S(1)}, bf16[1024,2,344]{0,2,1:T(8,128)(2,1)}, u32[]{:S(2)}) copy-start(bf16[1024,2,344]{0,2,1:T(8,128)(2,1)} %param.20) | copy-start | bytes 4227076
  6.5 101.5 %reduce-scatter.3.cloned.1.call-start = ((), (), s32[]{:S(2)}) async-start(), calls=%async_computation.2 | async-start | bytes 655360 | tf_op jit(solution)/shard_map/reduce_scatter | solution.py:87
  46.0 3.3 copy-start.6
  78.1 5.9 %copy-start.2 = (bf16[64,1024]{1,0:T(8,128)(2,1)S(1)}, bf16[64,1024]{1,0:T(8,128)(2,1)}, u32[]{:S(2)}) copy-start(bf16[64,1024]{1,0:T(8,128)(2,1)} %param.11) | copy-start | bytes 393220
  78.1 41.5 %copy-start.4 = (f32[1024]{0:T(1024)S(1)}, f32[1024]{0:T(1024)}, u32[]{:S(2)}) copy-start(f32[1024]{0:T(1024)} %param.19) | copy-start | bytes 12292
  83.9 80.1 %all-gather.6.cloned.1.call-start = ((), (), s32[]{:S(2)}) async-start(), calls=%async_computation.3 | async-start | bytes 4325376 | tf_op jit(solution)/shard_map/all_gather | solution.py:98
  121.3 156.3 %all-gather.8.cloned.1.call-start = ((), (), s32[]{:S(2)}) async-start(), calls=%async_computation.5 | async-start | bytes 14090240 | tf_op jit(solution)/shard_map/all_gather | solution.py:104
  170.8 238.6 %reduce-scatter.5.cloned.1.call-start = ((), (), s32[]{:S(2)}) async-start(), calls=%async_computation.4 | async-start | bytes 4325376 | tf_op jit(solution)/shard_map/reduce_scatter | solution.py:107
  319.0 2.6 copy-start.5
  321.7 89.3 %copy-start.1 = (bf16[1024,2,344]{0,2,1:T(8,128)(2,1)S(1)}, bf16[1024,2,344]{0,2,1:T(8,128)(2,1)}, u32[]{:S(2)}) copy-start(bf16[1024,2,344]{0,2,1:T(8,128)(2,1)} %param.20) | copy-start | bytes 4227076
  326.1 83.3 %copy-start.3 = (bf16[64,1024]{1,0:T(8,128)(2,1)S(1)}, bf16[64,1024]{1,0:T(8,128)(2,1)}, u32[]{:S(2)}) copy-start(bf16[64,1024]{1,0:T(8,128)(2,1)} %reduce-scatter.3.cloned.1.call-done) | copy-start | bytes 393220
Sparse Core Ops, SparseCore 0:
  84.0 20.4 reduce-scatter.2
  121.4 42.5 all-gather.5
  170.9 106.6 all-gather.7
  326.2 83.0 reduce-scatter.4
